TPU v7x, 128 devices: a whole 4x4x4 slice. The times are simulated.
128 devices in a mesh: sec: 2 (over y_hi), dev: 32 (over z, x, core), tp: 2 (over y_lo).
Axes of the slice: x: 4, y: 4 (y_hi: 2, y_lo: 2; y = y_hi * 2 + y_lo), z: 4, core: 2. Of those that a mesh axis runs over, the one named last changes fastest.
Arguments:
- queries: bfloat16 [512, 8192], P(('sec', 'dev'), 'tp'), may hold values from -6 to 6
- new_keys: bfloat16 [512, 1024], P(('sec', 'dev'), 'tp'), may hold values from -6 to 6
- token_values: bfloat16 [512, 1024], P(('sec', 'dev'), 'tp'), may hold values from -6 to 6
- key_cache: bfloat16 [512, 256, 1024], P(('sec', 'dev'), None, 'tp'), may hold values from -6 to 6
- stored_values: bfloat16 [512, 256, 1024], P(('sec', 'dev'), None, 'tp'), may hold values from -6 to 6
- cache_lengths: int32 [512], P(('sec', 'dev')), may hold values from 1 to 256, 65536 in all
- residual: bfloat16 [512, 8192], P(('sec', 'dev', 'tp')), may hold values from -6 to 6
- norm_gain: float32 [8192], replicated, may hold values from 0.25 to 1.75
- active: int32 [512, 16], P(('sec', 'dev', 'tp')), may hold values from 0 to 127, all different within a row; in each aligned block of 4 rows (0 to 3, 4 to 7, ...) at most 3 rows name the same one
- gate_weight: bfloat16 [8192, 16384], P(None, ('sec', 'dev', 'tp')), may hold values from -0.0625 to 0.0625
- up_weight: bfloat16 [8192, 16384], P(None, ('sec', 'dev', 'tp')), may hold values from -0.0625 to 0.0625
- down_weight: bfloat16 [16384, 8192], P(('sec', 'dev', 'tp')), may hold values from -0.125 to 0.125
Outputs:
- layer_out: bfloat16 [512, 8192], P(('sec', 'dev', 'tp'))
Inputs may be any that keep to these rules, and one draw needn't show every extreme that they name: `cache_lengths`: the largest length is 256 in every draw. `active`: the bundles of one row are distinct. Among the 4 rows of one device (aligned blocks of rows), no bundle is named by more than 3 rows, and some bundle reaches 3.
All inputs are finite; a program needn't handle non-finite values. No bound on the sum of `cache_lengths` on one device may be relied on, other than what follows from the above.
Results may differ from a plain program's by a relative error of at most 0.007.
Values may be sent and summed in bfloat16 or wider, within the bound.
A program may use at most 128 MiB of HBM per device.

v0:
```python
import jax
import jax.numpy as jnp
from jax import lax
from jax.sharding import PartitionSpec as P

HEAD_SIZE = 128
CACHE_POSITIONS = 256
epsilon = 1e-05


def attend(queries, new_keys, token_values, key_cache, stored_values, cache_lengths):
    request_count, query_width = queries.shape
    kv_width = new_keys.shape[1]
    kv_heads = kv_width // HEAD_SIZE
    group_width = query_width // kv_width
    scaling = HEAD_SIZE ** (-0.5)
    grouped = queries.reshape(request_count, kv_heads, group_width, HEAD_SIZE)
    cached_keys = key_cache.reshape(request_count, CACHE_POSITIONS, kv_heads, HEAD_SIZE)
    cached_values = stored_values.reshape(request_count, CACHE_POSITIONS, kv_heads, HEAD_SIZE)
    scores = (
        jnp.einsum("rkgd,rckd->rkgc", grouped, cached_keys, preferred_element_type=jnp.float32)
        * scaling
    )
    visible = jnp.arange(CACHE_POSITIONS, dtype=jnp.int32)[None, :] < cache_lengths[:, None]
    scores = jnp.where(visible[:, None, None, :], scores, -jnp.inf)
    fresh_keys = new_keys.reshape(request_count, kv_heads, HEAD_SIZE)
    fresh_score = (
        jnp.einsum("rkgd,rkd->rkg", grouped, fresh_keys, preferred_element_type=jnp.float32)
        * scaling
    )
    highest = jnp.maximum(jnp.max(scores, axis=-1), fresh_score)
    weights_cache = jnp.exp(scores - highest[..., None])
    weight_fresh = jnp.exp(fresh_score - highest)
    denominator = jnp.sum(weights_cache, axis=-1) + weight_fresh
    probs_cache = (weights_cache / denominator[..., None]).astype(jnp.bfloat16)
    prob_fresh = (weight_fresh / denominator).astype(jnp.bfloat16)
    blended = jnp.einsum(
        "rkgc,rckd->rkgd", probs_cache, cached_values, preferred_element_type=jnp.float32
    )
    fresh_values = token_values.reshape(request_count, kv_heads, 1, HEAD_SIZE).astype(jnp.float32)
    blended = blended + prob_fresh[..., None].astype(jnp.float32) * fresh_values
    return blended.reshape(request_count, query_width).astype(jnp.bfloat16)


def feed_forward(row_block, gate_weight, up_weight, selected):
    gate_value = jnp.dot(row_block, gate_weight, preferred_element_type=jnp.float32)
    up_value = jnp.dot(row_block, up_weight, preferred_element_type=jnp.float32)
    return (jax.nn.relu(gate_value) * up_value * selected).astype(jnp.bfloat16)


def shards(
    queries,
    new_keys,
    token_values,
    key_cache,
    stored_values,
    cache_lengths,
    residual,
    norm_gain,
    active,
    gate_weight,
    up_weight,
    down_weight,
):
    context = attend(queries, new_keys, token_values, key_cache, stored_values, cache_lengths)
    context = lax.all_to_all(context, "tp", split_axis=0, concat_axis=1, tiled=True)
    stream = residual.astype(jnp.float32) + context.astype(jnp.float32)
    mean_square = jnp.mean(stream * stream, axis=1, keepdims=True)
    normed = (stream * lax.rsqrt(mean_square + epsilon) * norm_gain[None, :]).astype(jnp.bfloat16)
    local_rows, model_width = normed.shape
    device_count = lax.axis_size(("sec", "dev", "tp"))
    top_count = active.shape[1]
    slot_limit = max(3, (2 * local_rows * top_count + device_count - 1) // device_count)
    targets = jnp.arange(device_count, dtype=jnp.int32)
    naming = jnp.any(active[:, :, None] == targets[None, None, :], axis=1).astype(jnp.int32)
    earlier = jnp.cumsum(naming, axis=0) - naming
    slot_ids = jnp.arange(slot_limit, dtype=jnp.int32)
    placed = (
        (naming.T[:, None, :] == 1) & (earlier.T[:, None, :] == slot_ids[None, :, None])
    ).astype(jnp.bfloat16)
    outgoing = jnp.einsum("bsr,rd->bsd", placed, normed, preferred_element_type=jnp.float32).astype(
        jnp.bfloat16
    )
    received = lax.all_to_all(
        outgoing, ("sec", "dev", "tp"), split_axis=0, concat_axis=0, tiled=True
    )
    slot_count = received.shape[1]
    flat_rows = received.reshape(device_count * slot_count, model_width)
    hidden = feed_forward(flat_rows, gate_weight, up_weight, 1.0)
    partial_terms = jnp.dot(hidden, down_weight, preferred_element_type=jnp.float32)
    partial_terms = partial_terms.reshape(device_count, slot_count, model_width)
    returned = lax.all_to_all(
        partial_terms.astype(jnp.bfloat16),
        ("sec", "dev", "tp"),
        split_axis=0,
        concat_axis=0,
        tiled=True,
    ).astype(partial_terms.dtype)
    update = jnp.einsum(
        "bsr,bsd->rd", placed.astype(jnp.float32), returned, precision=lax.Precision.HIGHEST
    )
    return (stream + update).astype(jnp.bfloat16)


def solution(mesh):
    return jax.shard_map(
        shards,
        mesh=mesh,
        in_specs=(
            P(("sec", "dev"), "tp"),
            P(("sec", "dev"), "tp"),
            P(("sec", "dev"), "tp"),
            P(("sec", "dev"), None, "tp"),
            P(("sec", "dev"), None, "tp"),
            P(("sec", "dev")),
            P(("sec", "dev", "tp"), None),
            P(),
            P(("sec", "dev", "tp"), None),
            P(None, ("sec", "dev", "tp")),
            P(None, ("sec", "dev", "tp")),
            P(("sec", "dev", "tp"), None),
        ),
        out_specs=P(("sec", "dev", "tp"), None),
        check_vma=False,
    )
```

profile of v0, /device:TPU:2, one launch (start us, length us, event | category | flops | bytes accessed | tf_op | source)
XLA Modules:
  0.0 301.2 jit_solution(82121312440829299)
XLA Ops:
  0.0 0.9 iota_compare_fusion.1
  0.9 0.8 bitcast_convert_fusion
  1.7 1.0 fusion.29
  2.7 2.4 fusion.43
  5.1 0.2 fusion.22
  5.3 0.0 copy-start.1
  5.4 0.0 copy-done.4
  5.4 0.0 copy-start.2
  5.4 0.5 fusion.19
  5.8 0.7 convert_element_type.74
  6.5 3.3 %all-to-all-start = ((bf16[2,4,4096]{2,1,0:T(4,128)(2,1)}), bf16[2,4,4096]{2,1,0:T(4,128)(2,1)S(1)}, u32[]{:S(2)}, u32[]{:S(2)}) async-start(bf16[2,4,4096]{2,1,0:T(4,128)(2,1)} %convert_element_type.74), calls=%async_computation | async-start | bytes 131072 | tf_op jit(solution)/shard_map/all_to_all | solution.py:66
  9.8 0.0 copy-done.3
  9.8 0.1 fusion.32
  10.0 3.9 %all-to-all-done = bf16[2,4,4096]{2,1,0:T(4,128)(2,1)S(1)} async-done(((bf16[2,4,4096]{2,1,0:T(4,128)(2,1)}), bf16[2,4,4096]{2,1,0:T(4,128)(2,1)S(1)}, u32[]{:S(2)}, u32[]{:S(2)}) %all-to-all-start) | async-done | bytes 65568 | tf_op jit(solution)/shard_map/all_to_all | solution.py:66
  13.9 0.2 multiply_reduce_fusion
  14.1 4.6 %convolution_convert_fusion.1 = bf16[128,3,8192]{2,0,1:T(8,128)(2,1)} fusion(f32[8192]{0:T(1024)S(1)} %copy-done.2, f32[4]{0:T(128)S(1)} %add_rsqrt_fusion, f32[4,8192]{1,0:T(4,128)S(1)} %bitcast.57, bf16[4,8192]{1,0:T(4,128)(2,1)S(1)} %copy-done.1, s32[128,4]{0,1:T(4,128)S(1)} %subtract_bitcast_fusion, pred[128,4]{0,1:T(4,128)(4,1)S(1)} %get-tuple-element.7), kind=kOutput, calls=%fused_computation.1 | convolution fusion | flops 28478464 | bytes 6523408 | tf_op jit(solution)/shard_map/bsr,rd->bsd/dot_general | solution.py:81
  18.7 11.4 %copy.34 = bf16[128,3,8192]{2,1,0:T(4,128)(2,1)} copy(bf16[128,3,8192]{2,0,1:T(8,128)(2,1)} %convolution_convert_fusion.1) | data formatting | bytes 12582912 | tf_op jit(solution)/shard_map/convert_element_type | solution.py:81
  30.1 112.5 %all_to_all.20 = bf16[128,3,8192]{2,1,0:T(4,128)(2,1)} all-to-all(bf16[128,3,8192]{2,1,0:T(4,128)(2,1)} %copy.34), channel_id=1, replica_groups=mesh['sec'=2,'dev'=32,'tp'=2] {'sec','dev','tp'}, dimensions={0} | all-to-all | bytes 12582912 | tf_op jit(solution)/shard_map/all_to_all | solution.py:84
  142.6 13.7 %reshape.73 = bf16[384,8192]{1,0:T(8,128)(2,1)} reshape(bf16[128,3,8192]{2,1,0:T(4,128)(2,1)} %all_to_all.20) | data formatting | bytes 12582912 | tf_op jit(solution)/shard_map/reshape | solution.py:88
  156.3 5.2 %convolution_maximum_fusion = f32[384,128]{1,0:T(8,128)S(1)} fusion(bf16[384,8192]{1,0:T(8,128)(2,1)} %reshape.73, bf16[8192,128]{1,0:T(8,128)(2,1)} %param.21), kind=kOutput, calls=%fused_computation.15 | convolution fusion | flops 805355520 | bytes 8585216 | tf_op jit(solution)/shard_map/dot_general | solution.py:46
  161.5 12.8 %convolution_convert_fusion = bf16[384,8192]{1,0:T(8,128)(2,1)} fusion(bf16[128,8192]{1,0:T(8,128)(2,1)S(1)} %copy-done, f32[384,128]{1,0:T(8,128)S(1)} %convolution_maximum_fusion, bf16[384,8192]{1,0:T(8,128)(2,1)} %reshape.73, bf16[8192,128]{1,0:T(8,128)(2,1)} %param.22), kind=kOutput, calls=%fused_computation | convolution fusion | flops 1613856768 | bytes 16973824 | tf_op jit(solution)/shard_map/dot_general | solution.py:90
  174.3 12.8 %convert_element_type.83 = bf16[128,3,8192]{2,1,0:T(4,128)(2,1)} reshape(bf16[384,8192]{1,0:T(8,128)(2,1)} %convolution_convert_fusion) | data formatting | bytes 12582912 | tf_op jit(solution)/shard_map/convert_element_type | solution.py:93
  187.1 106.7 %all_to_all.21 = bf16[128,3,8192]{2,1,0:T(4,128)(2,1)S(1)} all-to-all(bf16[128,3,8192]{2,1,0:T(4,128)(2,1)} %convert_element_type.83), channel_id=1, replica_groups=mesh['sec'=2,'dev'=32,'tp'=2] {'sec','dev','tp'}, dimensions={0} | all-to-all | bytes 12582912 | tf_op jit(solution)/shard_map/all_to_all | solution.py:92
  293.9 7.3 %fusion.1 = bf16[4,8192]{1,0:T(4,128)(2,1)} fusion(bf16[128,3,8192]{2,1,0:T(4,128)(2,1)S(1)} %all_to_all.21, f32[4,8192]{1,0:T(4,128)S(1)} %bitcast.58, bf16[4,8192]{1,0:T(4,128)(2,1)S(1)} %copy-done.1, s32[128,4]{0,1:T(4,128)S(1)} %subtract_bitcast_fusion, pred[128,4]{0,1:T(4,128)(4,1)S(1)} %get-tuple-element.7), kind=kOutput, calls=%fused_computation.4 | convolution fusion | flops 25299968 | bytes 6556160 | tf_op jit(solution)/shard_map/bsr,bsd->rd/dot_general | solution.py:99
  (14 shorter events, 0.1 us)
Async XLA Ops:
  0.0 161.5 %copy-start = (bf16[128,8192]{1,0:T(8,128)(2,1)S(1)}, bf16[128,8192]{1,0:T(8,128)(2,1)}, u32[]{:S(2)}) copy-start(bf16[128,8192]{1,0:T(8,128)(2,1)} %param.23) | copy-start | bytes 6291460
  0.0 5.4 %copy-start.4 = (bf16[8,256,512]{2,1,0:T(8,128)(2,1)S(1)}, bf16[8,256,512]{2,1,0:T(8,128)(2,1)}, u32[]{:S(2)}) copy-start(bf16[8,256,512]{2,1,0:T(8,128)(2,1)} %param.16) | copy-start | bytes 6291460
  5.1 4.7 %copy-start.3 = (s32[4,16]{1,0:T(4,128)S(1)}, s32[4,16]{1,0:T(4,128)}, u32[]{:S(2)}) copy-start(s32[4,16]{1,0:T(4,128)} %param.20) | copy-start | bytes 772
  5.3 8.6 %copy-start.1 = (bf16[4,8192]{1,0:T(4,128)(2,1)S(1)}, bf16[4,8192]{1,0:T(4,128)(2,1)}, u32[]{:S(2)}) copy-start(bf16[4,8192]{1,0:T(4,128)(2,1)} %param.18) | copy-start | bytes 196612
  5.4 8.8 %copy-start.2 = (f32[8192]{0:T(1024)S(1)}, f32[8192]{0:T(1024)}, u32[]{:S(2)}) copy-start(f32[8192]{0:T(1024)} %param.19) | copy-start | bytes 98308
  6.5 7.4 %all-to-all-start = ((bf16[2,4,4096]{2,1,0:T(4,128)(2,1)}), bf16[2,4,4096]{2,1,0:T(4,128)(2,1)S(1)}, u32[]{:S(2)}, u32[]{:S(2)}) async-start(bf16[2,4,4096]{2,1,0:T(4,128)(2,1)} %convert_element_type.74), calls=%async_computation | async-start | bytes 131072 | tf_op jit(solution)/shard_map/all_to_all | solution.py:66
where the time goes:
time: 302 us; the launch traced here: 301 us
  blocking collectives  219 us (73%)
  local copies, waits for them, and re-layouts  38.6 us (13%)
  matrix products  33.7 us (11%)
  waiting for transfers between devices  3.94 us (1%)
  starting transfers between devices  3.3 us (1%)
    all_to_all x1, blocking collectives, shards(): lax.all_to_all(outgoing, ('sec', 'dev', 'tp'), split_axis=0, concat_axis=...  113 us
    all_to_all x1, blocking collectives, shards(): lax.all_to_all(partial_terms.astype(jnp.bfloat16), ('sec', 'dev', 'tp'),...  107 us
    reshape x1, local copies, waits for them, and re-layouts, shards(): flat_rows = received.reshape(device_count * slot_count, model_width)  13.7 us
    convert_element_type x1, local copies, waits for them, and re-layouts, shards(): partial_terms.astype(jnp.bfloat16)  12.8 us
    dot_general x1, matrix products, shards(): jnp.dot(hidden, down_weight, preferred_element_type=jnp.float32)  12.8 us
    convert_element_type x1, local copies, waits for them, and re-layouts, shards(): jnp.einsum('bsr,rd->bsd', placed, normed, preferred_element_type=jnp.floa...  11.4 us
    dot_general x1, matrix products, shards(): jnp.einsum('bsr,bsd->rd', placed.astype(jnp.float32), returned, precision...  7.3 us
  transfers between devices with their start and end apart: 1, of which 1 were waited for; matrix products, arithmetic and copies ran while one was open for 0% of the time, Pallas kernels for 0%

commit v1 on v0

--- a/solution.py
+++ b/solution.py
@@ -63,7 +63,12 @@
     down_weight,
 ):
     context = attend(queries, new_keys, token_values, key_cache, stored_values, cache_lengths)
-    context = lax.all_to_all(context, "tp", split_axis=0, concat_axis=1, tiled=True)
+    context = jnp.concatenate(
+        lax.all_to_all(
+            jnp.stack(jnp.split(context, lax.axis_size("tp"), axis=0), axis=0), "tp", 0, 0
+        ),
+        axis=1,
+    )
     stream = residual.astype(jnp.float32) + context.astype(jnp.float32)
     mean_square = jnp.mean(stream * stream, axis=1, keepdims=True)
     normed = (stream * lax.rsqrt(mean_square + epsilon) * norm_gain[None, :]).astype(jnp.bfloat16)

time: 302 us -> 302 us (level)
  no operation moved by 1% of the time
where the time goes in v1:
time: 302 us; the launch traced here: 301 us
  blocking collectives  219 us (73%)
  local copies, waits for them, and re-layouts  38 us (13%)
  matrix products  33.7 us (11%)
  waiting for transfers between devices  3.94 us (1%)
  starting transfers between devices  3.3 us (1%)
    all_to_all x1, blocking collectives, shards(): lax.all_to_all(outgoing, ('sec', 'dev', 'tp'), split_axis=0, concat_axis=...  113 us
    all_to_all x1, blocking collectives, shards(): lax.all_to_all(partial_terms.astype(jnp.bfloat16), ('sec', 'dev', 'tp'),...  107 us
    reshape x1, local copies, waits for them, and re-layouts, shards(): flat_rows = received.reshape(device_count * slot_count, model_width)  13.7 us
    convert_element_type x1, local copies, waits for them, and re-layouts, shards(): partial_terms.astype(jnp.bfloat16)  12.8 us
    dot_general x1, matrix products, shards(): jnp.dot(hidden, down_weight, preferred_element_type=jnp.float32)  12.8 us
    convert_element_type x1, local copies, waits for them, and re-layouts, shards(): jnp.einsum('bsr,rd->bsd', placed, normed, preferred_element_type=jnp.floa...  11.4 us
    dot_general x1, matrix products, shards(): jnp.einsum('bsr,bsd->rd', placed.astype(jnp.float32), returned, precision...  7.3 us
  transfers between devices with their start and end apart: 1, of which 1 were waited for; matrix products, arithmetic and copies ran while one was open for 0% of the time, Pallas kernels for 0%

profile of v1, /device:TPU:2, one launch (start us, length us, event | category | flops | bytes accessed | tf_op | source)
XLA Modules:
  0.0 301.2 jit_solution(1741247206189230547)
XLA Ops:
  0.0 0.9 iota_compare_fusion.1
  0.9 0.8 bitcast_convert_fusion
  1.7 1.0 fusion.29
  2.7 2.4 fusion.44
  5.1 0.2 fusion.22
  5.3 0.0 copy-start.3
  5.4 0.0 copy-start.1
  5.4 0.0 copy-start.2
  5.4 0.5 fusion.19
  5.9 0.7 pad_maximum_fusion
  6.6 3.3 %all-to-all-start = ((bf16[2,4,4096]{2,1,0:T(4,128)(2,1)}), bf16[2,4,4096]{2,1,0:T(4,128)(2,1)S(1)}, u32[]{:S(2)}, u32[]{:S(2)}) async-start(bf16[2,4,4096]{2,1,0:T(4,128)(2,1)} %pad_maximum_fusion), calls=%async_computation | async-start | bytes 131072 | tf_op jit(solution)/shard_map/all_to_all | solution.py:67
  9.9 0.1 fusion.32
  10.0 3.9 %all-to-all-done = bf16[2,4,4096]{2,1,0:T(4,128)(2,1)S(1)} async-done(((bf16[2,4,4096]{2,1,0:T(4,128)(2,1)}), bf16[2,4,4096]{2,1,0:T(4,128)(2,1)S(1)}, u32[]{:S(2)}, u32[]{:S(2)}) %all-to-all-start) | async-done | bytes 65568 | tf_op jit(solution)/shard_map/all_to_all | solution.py:67
  14.0 0.2 multiply_reduce_fusion
  14.2 0.0 copy-done.2
  14.2 4.6 %convolution_convert_fusion.1 = bf16[128,3,8192]{2,0,1:T(8,128)(2,1)} fusion(f32[8192]{0:T(1024)S(1)} %copy-done.2, f32[4]{0:T(128)S(1)} %add_rsqrt_fusion, f32[4,8192]{1,0:T(4,128)S(1)} %bitcast.59, bf16[4,8192]{1,0:T(4,128)(2,1)S(1)} %copy-done.1, s32[128,4]{0,1:T(4,128)S(1)} %subtract_bitcast_fusion, pred[128,4]{0,1:T(4,128)(4,1)S(1)} %get-tuple-element.9), kind=kOutput, calls=%fused_computation.1 | convolution fusion | flops 28478464 | bytes 6523408 | tf_op jit(solution)/shard_map/bsr,rd->bsd/dot_general | solution.py:86
  18.8 11.4 %copy.34 = bf16[128,3,8192]{2,1,0:T(4,128)(2,1)} copy(bf16[128,3,8192]{2,0,1:T(8,128)(2,1)} %convolution_convert_fusion.1) | data formatting | bytes 12582912 | tf_op jit(solution)/shard_map/convert_element_type | solution.py:86
  30.2 112.5 %all_to_all.15 = bf16[128,3,8192]{2,1,0:T(4,128)(2,1)} all-to-all(bf16[128,3,8192]{2,1,0:T(4,128)(2,1)} %copy.34), channel_id=1, replica_groups=mesh['sec'=2,'dev'=32,'tp'=2] {'sec','dev','tp'}, dimensions={0} | all-to-all | bytes 12582912 | tf_op jit(solution)/shard_map/all_to_all | solution.py:89
  142.7 13.7 %reshape.75 = bf16[384,8192]{1,0:T(8,128)(2,1)} reshape(bf16[128,3,8192]{2,1,0:T(4,128)(2,1)} %all_to_all.15) | data formatting | bytes 12582912 | tf_op jit(solution)/shard_map/reshape | solution.py:93
  156.4 5.2 %convolution_maximum_fusion = f32[384,128]{1,0:T(8,128)S(1)} fusion(bf16[384,8192]{1,0:T(8,128)(2,1)} %reshape.75, bf16[8192,128]{1,0:T(8,128)(2,1)} %param.21), kind=kOutput, calls=%fused_computation.15 | convolution fusion | flops 805355520 | bytes 8585216 | tf_op jit(solution)/shard_map/dot_general | solution.py:46
  161.6 12.8 %convolution_convert_fusion = bf16[384,8192]{1,0:T(8,128)(2,1)} fusion(bf16[128,8192]{1,0:T(8,128)(2,1)S(1)} %copy-done, f32[384,128]{1,0:T(8,128)S(1)} %convolution_maximum_fusion, bf16[384,8192]{1,0:T(8,128)(2,1)} %reshape.75, bf16[8192,128]{1,0:T(8,128)(2,1)} %param.22), kind=kOutput, calls=%fused_computation | convolution fusion | flops 1613856768 | bytes 16973824 | tf_op jit(solution)/shard_map/dot_general | solution.py:95
  174.4 12.8 %convert_element_type.79 = bf16[128,3,8192]{2,1,0:T(4,128)(2,1)} reshape(bf16[384,8192]{1,0:T(8,128)(2,1)} %convolution_convert_fusion) | data formatting | bytes 12582912 | tf_op jit(solution)/shard_map/convert_element_type | solution.py:98
  187.2 106.7 %all_to_all.16 = bf16[128,3,8192]{2,1,0:T(4,128)(2,1)S(1)} all-to-all(bf16[128,3,8192]{2,1,0:T(4,128)(2,1)} %convert_element_type.79), channel_id=1, replica_groups=mesh['sec'=2,'dev'=32,'tp'=2] {'sec','dev','tp'}, dimensions={0} | all-to-all | bytes 12582912 | tf_op jit(solution)/shard_map/all_to_all | solution.py:97
  293.9 7.3 %fusion.1 = bf16[4,8192]{1,0:T(4,128)(2,1)} fusion(bf16[128,3,8192]{2,1,0:T(4,128)(2,1)S(1)} %all_to_all.16, f32[4,8192]{1,0:T(4,128)S(1)} %bitcast.60, bf16[4,8192]{1,0:T(4,128)(2,1)S(1)} %copy-done.1, s32[128,4]{0,1:T(4,128)S(1)} %subtract_bitcast_fusion, pred[128,4]{0,1:T(4,128)(4,1)S(1)} %get-tuple-element.9), kind=kOutput, calls=%fused_computation.4 | convolution fusion | flops 25299968 | bytes 6556160 | tf_op jit(solution)/shard_map/bsr,bsd->rd/dot_general | solution.py:104
  (17 shorter events, 0.2 us)
Async XLA Ops:
  0.0 161.6 %copy-start = (bf16[128,8192]{1,0:T(8,128)(2,1)S(1)}, bf16[128,8192]{1,0:T(8,128)(2,1)}, u32[]{:S(2)}) copy-start(bf16[128,8192]{1,0:T(8,128)(2,1)} %param.23) | copy-start | bytes 6291460
  0.0 5.3 %copy-start.4 = (bf16[8,256,512]{2,1,0:T(8,128)(2,1)S(1)}, bf16[8,256,512]{2,1,0:T(8,128)(2,1)}, u32[]{:S(2)}) copy-start(bf16[8,256,512]{2,1,0:T(8,128)(2,1)} %param.16) | copy-start | bytes 6291460
  5.3 4.6 %copy-start.3 = (s32[4,16]{1,0:T(4,128)S(1)}, s32[4,16]{1,0:T(4,128)}, u32[]{:S(2)}) copy-start(s32[4,16]{1,0:T(4,128)} %param.20) | copy-start | bytes 772
  5.4 8.6 %copy-start.1 = (bf16[4,8192]{1,0:T(4,128)(2,1)S(1)}, bf16[4,8192]{1,0:T(4,128)(2,1)}, u32[]{:S(2)}) copy-start(bf16[4,8192]{1,0:T(4,128)(2,1)} %param.18) | copy-start | bytes 196612
  5.4 8.8 %copy-start.2 = (f32[8192]{0:T(1024)S(1)}, f32[8192]{0:T(1024)}, u32[]{:S(2)}) copy-start(f32[8192]{0:T(1024)} %param.19) | copy-start | bytes 98308
  6.6 7.4 %all-to-all-start = ((bf16[2,4,4096]{2,1,0:T(4,128)(2,1)}), bf16[2,4,4096]{2,1,0:T(4,128)(2,1)S(1)}, u32[]{:S(2)}, u32[]{:S(2)}) async-start(bf16[2,4,4096]{2,1,0:T(4,128)(2,1)} %pad_maximum_fusion), calls=%async_computation | async-start | bytes 131072 | tf_op jit(solution)/shard_map/all_to_all | solution.py:67
